TPU v7x, 256 devices: a whole 4x4x8 slice. The times are simulated.
256 devices in a mesh: tm: 4 (over y), space: 64 (over x, z, core).
Axes of the slice: x: 4, y: 4, z: 8, core: 2. Of those that a mesh axis runs over, the one named last changes fastest.
Arguments:
- queries: bfloat16 [16, 4096, 1536], P('tm', 'space'), may hold values from -48 to 48
- key_rows: bfloat16 [16, 4096, 1536], P('tm', 'space'), may hold values from -4 to 4
- value_rows: bfloat16 [16, 4096, 1536], P('tm', 'space'), may hold values from -6 to 6
- dropout: int32 [4, 16, 4096, 12], P(None, 'tm', 'space'), may hold values 0 or 1
- tile_lists: int32 [64, 2], P('space'), may hold values from 0 to 63, as said below
Outputs:
- sampled_heads: bfloat16 [4, 16, 4096, 1536], P(None, 'tm', 'space')
Inputs may be any that keep to these rules, and one draw needn't show every extreme that they name: `tile_lists`: row t holds t first and then (t - 1) or (t + 1) modulo 64.
All inputs are finite; a program needn't handle non-finite values. No bound on the sum of `dropout` on one device may be relied on, other than what follows from the above.
Results may differ from a plain program's by a relative error of at most 0.0045.
Values may be sent and summed in bfloat16 or wider, within the bound.
No kernel may reach another device: no remote copies, remote signals or barrier semaphores. Data moves between devices by JAX's collectives and lax.ppermute only.
A program may use at most 128 MiB of HBM per device.

v0:
```python
import math
import jax
import jax.numpy as jnp
from jax import lax
from jax.sharding import PartitionSpec as P

keep_rate = 0.9


def from_behind(shard, axis, by):
    peers = lax.axis_size(axis)
    return lax.ppermute(shard, axis, [(i, (i + by) % peers) for i in range(peers)])


def per_device(queries, key_rows, value_rows, dropout, tile_lists):
    frame_dev, tile_tok, width = queries.shape
    samples = dropout.shape[0]
    head_count = dropout.shape[3]
    head_dim = width // head_count
    factor = 1.0 / math.sqrt(head_dim)
    space_size = lax.axis_size("space")
    tile_here = lax.axis_index("space")
    span_here = lax.axis_index("tm")
    listed = tile_lists[0]
    drop_low = dropout.astype(jnp.bfloat16)
    all_keys, all_values, all_drops = (
        lax.all_gather(key_rows, "tm", axis=0, tiled=True),
        lax.all_gather(value_rows, "tm", axis=0, tiled=True),
        lax.all_gather(drop_low, "tm", axis=1, tiled=True),
    )
    key_parts = [all_keys]
    value_parts = [all_values]
    drop_parts = [all_drops]
    tile_ids = [tile_here]
    for offset in (1, -1):
        moved_keys, moved_values, moved_drops = from_behind(
            (all_keys, all_values, all_drops), "space", offset
        )
        key_parts.append(moved_keys)
        value_parts.append(moved_values)
        drop_parts.append(moved_drops)
        tile_ids.append((tile_here - offset) % space_size)
    window_keys = jnp.stack(key_parts, axis=1)
    window_values = jnp.stack(value_parts, axis=1)
    window_drops = jnp.stack(drop_parts, axis=2)
    tile_valid = jnp.stack([jnp.any(listed == ident) for ident in tile_ids])
    frames_all = window_keys.shape[0]
    window_count = window_keys.shape[1]
    key_total = frames_all * window_count * tile_tok
    key_flat = window_keys.reshape(key_total, width)
    value_flat = window_values.reshape(key_total, width)
    drop_heads = window_drops.reshape(samples, key_total, head_count).transpose(2, 0, 1)
    key_frame = jnp.repeat(jnp.arange(frames_all, dtype=jnp.int32), window_count * tile_tok)
    key_valid = jnp.tile(jnp.repeat(tile_valid, tile_tok), frames_all)
    query_frame = span_here * frame_dev + jnp.repeat(
        jnp.arange(frame_dev, dtype=jnp.int32), tile_tok
    )
    query_block = queries.reshape(frame_dev * tile_tok, width)
    key_limit = frames_all * window_count * tile_tok
    row_count = query_block.shape[0]
    allowed = (key_frame[None, :key_limit] <= query_frame[:, None]) & key_valid[None, :key_limit]

    def one_head(head, output):
        start = head * head_dim
        query_h = lax.dynamic_slice_in_dim(query_block, start, head_dim, 1)
        key_h = lax.dynamic_slice_in_dim(key_flat, start, head_dim, 1)
        value_h = lax.dynamic_slice_in_dim(value_flat, start, head_dim, 1)
        drop_h = lax.dynamic_index_in_dim(drop_heads, head, 0, keepdims=False)
        scores = (
            jnp.einsum("rd,kd->rk", query_h, key_h, preferred_element_type=jnp.float32) * factor
        )
        masked = jnp.where(allowed, scores, -1e30)
        highest = jnp.max(masked, axis=1, keepdims=True)
        weight = jnp.exp(masked - highest)
        total = jnp.sum(weight, axis=1)
        weight_low = weight.astype(jnp.bfloat16)
        dropped = weight_low[None] * drop_h[:, None, :]
        summed = jnp.einsum("srk,kd->srd", dropped, value_h, preferred_element_type=jnp.float32)
        result = (summed / (keep_rate * total)[None, :, None]).astype(jnp.bfloat16)
        return lax.dynamic_update_slice_in_dim(output, result, start, 2)

    initial = jnp.zeros((samples, row_count, width), jnp.bfloat16)
    output = lax.fori_loop(0, head_count, one_head, initial)
    return output.reshape(samples, frame_dev, tile_tok, width)


def solution(mesh):
    placed = (
        P("tm", "space", None),
        P("tm", "space", None),
        P("tm", "space", None),
        P(None, "tm", "space", None),
        P("space", None),
    )
    return jax.shard_map(
        per_device,
        mesh=mesh,
        in_specs=placed,
        out_specs=P(None, "tm", "space", None),
        check_vma=False,
    )
```

profile of v0, /device:TPU:97, one launch (start us, length us, event | category | flops | bytes accessed | tf_op | source)
XLA Modules:
  0.0 245.5 jit_solution(12780342836422055700)
XLA Ops:
  6.5 0.7 all-gather.5.cloned.1.call-update
  7.3 0.7 all-gather.3.cloned.1.call-update
  8.0 44.9 %all-gather.5.cloned.1.call-done = bf16[16,64,1536]{2,1,0:T(8,128)(2,1)} async-done(((bf16[4,64,1536]{2,1,0:T(8,128)(2,1)}), bf16[16,64,1536]{2,1,0:T(8,128)(2,1)}) %all-gather.5.cloned.1.call-update) | async-done | bytes 3145744 | tf_op jit(solution)/shard_map/all_gather | solution.py:28
  52.9 3.2 %collective-permute-start.4 = (bf16[16,64,1536]{2,1,0:T(8,128)(2,1)}, bf16[16,64,1536]{2,1,0:T(8,128)(2,1)S(1)}, u32[]{:S(2)}, u32[]{:S(2)}) collective-permute-start(bf16[16,64,1536]{2,1,0:T(8,128)(2,1)} %all-gather.5.cloned.1.call-done), channel_id=1, source_target_pairs={{0,1},{1,2},{2,3},{3,4},{4,5},{5,6},{6,7},{7,8},{8,9},{9,10},{10,1... | collective-permute-start | bytes 9437192 | tf_op jit(solution)/shard_map/ppermute | solution.py:12
  56.2 40.9 %all-gather.3.cloned.1.call-done = bf16[16,64,1536]{2,1,0:T(8,128)(2,1)} async-done(((bf16[4,64,1536]{2,1,0:T(8,128)(2,1)}), bf16[16,64,1536]{2,1,0:T(8,128)(2,1)}) %all-gather.3.cloned.1.call-update) | async-done | bytes 3145744 | tf_op jit(solution)/shard_map/all_gather | solution.py:27
  97.0 3.2 %collective-permute-start = (bf16[16,64,1536]{2,1,0:T(8,128)(2,1)}, bf16[16,64,1536]{2,1,0:T(8,128)(2,1)}, u32[]{:S(2)}, u32[]{:S(2)}) collective-permute-start(bf16[16,64,1536]{2,1,0:T(8,128)(2,1)} %all-gather.3.cloned.1.call-done), channel_id=1, source_target_pairs={{0,1},{1,2},{2,3},{3,4},{4,5},{5,6},{6,7},{7,8},{8,9},{9,10},{10,1... | collective-permute-start | bytes 9437192 | tf_op jit(solution)/shard_map/ppermute | solution.py:12
  100.3 0.9 copy_convert_fusion
  101.2 9.6 %all_gather.10 = bf16[4,16,64,12]{2,0,3,1:T(4,128)(2,1)S(1)} all-gather(bf16[4,4,64,12]{2,0,3,1:T(4,128)(2,1)S(1)} %copy_convert_fusion), channel_id=1, replica_groups=mesh['tm'=4,'space'=64] {'tm'}, dimensions={1}, use_global_device_ids=true | all-gather | bytes 122880 | tf_op jit(solution)/shard_map/all_gather | solution.py:29
  110.8 5.5 %collective-permute-start.2 = (bf16[4,16,64,12]{2,0,3,1:T(4,128)(2,1)S(1)}, bf16[4,16,64,12]{2,0,3,1:T(4,128)(2,1)S(1)}, u32[]{:S(2)}, u32[]{:S(2)}) collective-permute-start(bf16[4,16,64,12]{2,0,3,1:T(4,128)(2,1)S(1)} %all_gather.10), channel_id=1, source_target_pairs={{0,1},{1,2},{2,3},{3,4},{4,5},{5,6},{6,7},{7,8},{8,9},{9,10},{10,1... | collective-permute-start | bytes 294920 | tf_op jit(solution)/shard_map/ppermute | solution.py:12
  116.3 1.4 compare_reduce_fusion.2
  117.7 2.0 pad_add_fusion
  119.8 0.1 tile.7
  119.9 0.7 and.23
  120.6 16.2 %collective-permute-done.2 = bf16[4,16,64,12]{2,0,3,1:T(4,128)(2,1)S(1)} collective-permute-done((bf16[4,16,64,12]{2,0,3,1:T(4,128)(2,1)S(1)}, bf16[4,16,64,12]{2,0,3,1:T(4,128)(2,1)S(1)}, u32[]{:S(2)}, u32[]{:S(2)}) %collective-permute-start.2) | collective-permute-done | bytes 98336 | tf_op jit(solution)/shard_map/ppermute | solution.py:12
  136.8 0.1 collective-permute-start.3
  136.9 0.7 add.56
  137.6 0.7 le.15
  138.2 5.7 %collective-permute-done.3 = bf16[4,16,64,12]{2,0,3,1:T(4,128)(2,1)} collective-permute-done((bf16[4,16,64,12]{2,0,3,1:T(4,128)(2,1)S(1)}, bf16[4,16,64,12]{2,0,3,1:T(4,128)(2,1)}, u32[]{:S(2)}, u32[]{:S(2)}) %collective-permute-start.3) | collective-permute-done | bytes 98336 | tf_op jit(solution)/shard_map/ppermute | solution.py:12
  143.9 1.5 pad_maximum_fusion.2
  145.4 1.4 copy.15
  146.8 1.8 reshape.43
  148.6 1.6 copy-done.1
  150.3 8.5 %pad_maximum_fusion.1 = bf16[16,3,64,1536]{3,2,1,0:T(8,128)(2,1)} fusion(bf16[16,1,64,1536]{3,2,1,0:T(8,128)(2,1)} %bitcast.11, bf16[16,1,64,1536]{3,2,1,0:T(8,128)(2,1)} %bitcast.32, bf16[16,1,64,1536]{3,2,1,0:T(8,128)(2,1)} %bitcast.31), kind=kLoop, calls=%fused_computation.22 | loop fusion | flops 9437184 | bytes 18874368 | tf_op jit(solution)/shard_map/stack | solution.py:44
  158.8 6.9 %pad_maximum_fusion = bf16[16,3,64,1536]{3,2,1,0:T(8,128)(2,1)} fusion(bf16[16,1,64,1536]{3,2,1,0:T(8,128)(2,1)} %bitcast.3, bf16[16,1,64,1536]{3,2,1,0:T(8,128)(2,1)} %bitcast.2, bf16[16,1,64,1536]{3,2,1,0:T(8,128)(2,1)S(1)} %bitcast.30), kind=kLoop, calls=%fused_computation.21 | loop fusion | flops 9437184 | bytes 18874368 | tf_op jit(solution)/shard_map/stack | solution.py:43
  165.7 0.2 broadcast_in_dim.33
  166.0 0.5 copy-done.3
  166.4 70.5 %while.14 = (s32[]{:T(128)}, bf16[4,256,1536]{2,1,0:T(8,128)(2,1)S(1)}, bf16[256,1536]{1,0:T(8,128)(2,1)}, bf16[3072,1536]{1,0:T(8,128)(2,1)}, bf16[12,4,3072]{2...) while((s32[]{:T(128)}, ...), condition=%wide.region_6.7_spmd.clone, body=%wide.region_3.6_spmd.clone.sunk | while | flops 1016332032 | bytes 11436207 | solution.py:83
  166.4 2.2 fusion.32
  168.6 0.6 fusion.33
  169.3 3.0 %fusion.34 = bf16[4,256,1536]{2,1,0:T(8,128)(2,1)S(1)} fusion(bf16[4,256,1536]{2,1,0:T(8,128)(2,1)S(1)} %get-tuple-element.255, s32[]{:T(128)S(6)} %select_n.41, bf16[4,3072]{1,0:T(4,128)(2,1)S(1)} %dynamic-slice_bitcast_fusion.2, bf16[256,3072]{1,0:T(8,128)(2,1)S(1)} %get-tuple-element.239, bf16[3072,1536]{1,0:T(8,128)(2,1)} %get-tuple-element.272, ...), kind=kOutput, calls=%fused_computation.12.clone.1 | convolution fusion | flops 808714240 | bytes 2648064 | tf_op jit(solution)/shard_map/while/body/eval_jaxpr/srk,kd->srd/dot_general | solution.py:78
  172.3 2.2 fusion.32
  174.5 0.6 fusion.33
  175.1 3.0 %fusion.34 = bf16[4,256,1536]{2,1,0:T(8,128)(2,1)S(1)} fusion(bf16[4,256,1536]{2,1,0:T(8,128)(2,1)S(1)} %get-tuple-element.255, s32[]{:T(128)S(6)} %select_n.41, bf16[4,3072]{1,0:T(4,128)(2,1)S(1)} %dynamic-slice_bitcast_fusion.2, bf16[256,3072]{1,0:T(8,128)(2,1)S(1)} %get-tuple-element.239, bf16[3072,1536]{1,0:T(8,128)(2,1)} %get-tuple-element.272, ...), kind=kOutput, calls=%fused_computation.12.clone.1 | convolution fusion | flops 808714240 | bytes 2648064 | tf_op jit(solution)/shard_map/while/body/eval_jaxpr/srk,kd->srd/dot_general | solution.py:78
  178.2 2.2 fusion.32
  180.4 0.6 fusion.33
  181.0 3.0 %fusion.34 = bf16[4,256,1536]{2,1,0:T(8,128)(2,1)S(1)} fusion(bf16[4,256,1536]{2,1,0:T(8,128)(2,1)S(1)} %get-tuple-element.255, s32[]{:T(128)S(6)} %select_n.41, bf16[4,3072]{1,0:T(4,128)(2,1)S(1)} %dynamic-slice_bitcast_fusion.2, bf16[256,3072]{1,0:T(8,128)(2,1)S(1)} %get-tuple-element.239, bf16[3072,1536]{1,0:T(8,128)(2,1)} %get-tuple-element.272, ...), kind=kOutput, calls=%fused_computation.12.clone.1 | convolution fusion | flops 808714240 | bytes 2648064 | tf_op jit(solution)/shard_map/while/body/eval_jaxpr/srk,kd->srd/dot_general | solution.py:78
  184.1 2.2 fusion.32
  186.2 0.6 fusion.33
  186.9 3.0 %fusion.34 = bf16[4,256,1536]{2,1,0:T(8,128)(2,1)S(1)} fusion(bf16[4,256,1536]{2,1,0:T(8,128)(2,1)S(1)} %get-tuple-element.255, s32[]{:T(128)S(6)} %select_n.41, bf16[4,3072]{1,0:T(4,128)(2,1)S(1)} %dynamic-slice_bitcast_fusion.2, bf16[256,3072]{1,0:T(8,128)(2,1)S(1)} %get-tuple-element.239, bf16[3072,1536]{1,0:T(8,128)(2,1)} %get-tuple-element.272, ...), kind=kOutput, calls=%fused_computation.12.clone.1 | convolution fusion | flops 808714240 | bytes 2648064 | tf_op jit(solution)/shard_map/while/body/eval_jaxpr/srk,kd->srd/dot_general | solution.py:78
  189.9 2.2 fusion.32
  192.1 0.6 fusion.33
  192.8 3.0 %fusion.34 = bf16[4,256,1536]{2,1,0:T(8,128)(2,1)S(1)} fusion(bf16[4,256,1536]{2,1,0:T(8,128)(2,1)S(1)} %get-tuple-element.255, s32[]{:T(128)S(6)} %select_n.41, bf16[4,3072]{1,0:T(4,128)(2,1)S(1)} %dynamic-slice_bitcast_fusion.2, bf16[256,3072]{1,0:T(8,128)(2,1)S(1)} %get-tuple-element.239, bf16[3072,1536]{1,0:T(8,128)(2,1)} %get-tuple-element.272, ...), kind=kOutput, calls=%fused_computation.12.clone.1 | convolution fusion | flops 808714240 | bytes 2648064 | tf_op jit(solution)/shard_map/while/body/eval_jaxpr/srk,kd->srd/dot_general | solution.py:78
  195.8 2.2 fusion.32
  198.0 0.6 fusion.33
  198.6 3.0 %fusion.34 = bf16[4,256,1536]{2,1,0:T(8,128)(2,1)S(1)} fusion(bf16[4,256,1536]{2,1,0:T(8,128)(2,1)S(1)} %get-tuple-element.255, s32[]{:T(128)S(6)} %select_n.41, bf16[4,3072]{1,0:T(4,128)(2,1)S(1)} %dynamic-slice_bitcast_fusion.2, bf16[256,3072]{1,0:T(8,128)(2,1)S(1)} %get-tuple-element.239, bf16[3072,1536]{1,0:T(8,128)(2,1)} %get-tuple-element.272, ...), kind=kOutput, calls=%fused_computation.12.clone.1 | convolution fusion | flops 808714240 | bytes 2648064 | tf_op jit(solution)/shard_map/while/body/eval_jaxpr/srk,kd->srd/dot_general | solution.py:78
  201.7 2.2 fusion.32
  203.9 0.6 fusion.33
  204.5 3.0 %fusion.34 = bf16[4,256,1536]{2,1,0:T(8,128)(2,1)S(1)} fusion(bf16[4,256,1536]{2,1,0:T(8,128)(2,1)S(1)} %get-tuple-element.255, s32[]{:T(128)S(6)} %select_n.41, bf16[4,3072]{1,0:T(4,128)(2,1)S(1)} %dynamic-slice_bitcast_fusion.2, bf16[256,3072]{1,0:T(8,128)(2,1)S(1)} %get-tuple-element.239, bf16[3072,1536]{1,0:T(8,128)(2,1)} %get-tuple-element.272, ...), kind=kOutput, calls=%fused_computation.12.clone.1 | convolution fusion | flops 808714240 | bytes 2648064 | tf_op jit(solution)/shard_map/while/body/eval_jaxpr/srk,kd->srd/dot_general | solution.py:78
  207.6 2.2 fusion.32
  209.7 0.6 fusion.33
  210.4 3.0 %fusion.34 = bf16[4,256,1536]{2,1,0:T(8,128)(2,1)S(1)} fusion(bf16[4,256,1536]{2,1,0:T(8,128)(2,1)S(1)} %get-tuple-element.255, s32[]{:T(128)S(6)} %select_n.41, bf16[4,3072]{1,0:T(4,128)(2,1)S(1)} %dynamic-slice_bitcast_fusion.2, bf16[256,3072]{1,0:T(8,128)(2,1)S(1)} %get-tuple-element.239, bf16[3072,1536]{1,0:T(8,128)(2,1)} %get-tuple-element.272, ...), kind=kOutput, calls=%fused_computation.12.clone.1 | convolution fusion | flops 808714240 | bytes 2648064 | tf_op jit(solution)/shard_map/while/body/eval_jaxpr/srk,kd->srd/dot_general | solution.py:78
  213.5 2.2 fusion.32
  215.6 0.6 fusion.33
  216.3 3.0 %fusion.34 = bf16[4,256,1536]{2,1,0:T(8,128)(2,1)S(1)} fusion(bf16[4,256,1536]{2,1,0:T(8,128)(2,1)S(1)} %get-tuple-element.255, s32[]{:T(128)S(6)} %select_n.41, bf16[4,3072]{1,0:T(4,128)(2,1)S(1)} %dynamic-slice_bitcast_fusion.2, bf16[256,3072]{1,0:T(8,128)(2,1)S(1)} %get-tuple-element.239, bf16[3072,1536]{1,0:T(8,128)(2,1)} %get-tuple-element.272, ...), kind=kOutput, calls=%fused_computation.12.clone.1 | convolution fusion | flops 808714240 | bytes 2648064 | tf_op jit(solution)/shard_map/while/body/eval_jaxpr/srk,kd->srd/dot_general | solution.py:78
  219.3 2.2 fusion.32
  221.5 0.6 fusion.33
  222.2 3.0 %fusion.34 = bf16[4,256,1536]{2,1,0:T(8,128)(2,1)S(1)} fusion(bf16[4,256,1536]{2,1,0:T(8,128)(2,1)S(1)} %get-tuple-element.255, s32[]{:T(128)S(6)} %select_n.41, bf16[4,3072]{1,0:T(4,128)(2,1)S(1)} %dynamic-slice_bitcast_fusion.2, bf16[256,3072]{1,0:T(8,128)(2,1)S(1)} %get-tuple-element.239, bf16[3072,1536]{1,0:T(8,128)(2,1)} %get-tuple-element.272, ...), kind=kOutput, calls=%fused_computation.12.clone.1 | convolution fusion | flops 808714240 | bytes 2648064 | tf_op jit(solution)/shard_map/while/body/eval_jaxpr/srk,kd->srd/dot_general | solution.py:78
  225.2 2.2 fusion.32
  227.4 0.6 fusion.33
  228.0 3.0 %fusion.34 = bf16[4,256,1536]{2,1,0:T(8,128)(2,1)S(1)} fusion(bf16[4,256,1536]{2,1,0:T(8,128)(2,1)S(1)} %get-tuple-element.255, s32[]{:T(128)S(6)} %select_n.41, bf16[4,3072]{1,0:T(4,128)(2,1)S(1)} %dynamic-slice_bitcast_fusion.2, bf16[256,3072]{1,0:T(8,128)(2,1)S(1)} %get-tuple-element.239, bf16[3072,1536]{1,0:T(8,128)(2,1)} %get-tuple-element.272, ...), kind=kOutput, calls=%fused_computation.12.clone.1 | convolution fusion | flops 808714240 | bytes 2648064 | tf_op jit(solution)/shard_map/while/body/eval_jaxpr/srk,kd->srd/dot_general | solution.py:78
  231.1 2.2 fusion.32
  233.3 0.6 fusion.33
  233.9 3.0 %fusion.34 = bf16[4,256,1536]{2,1,0:T(8,128)(2,1)S(1)} fusion(bf16[4,256,1536]{2,1,0:T(8,128)(2,1)S(1)} %get-tuple-element.255, s32[]{:T(128)S(6)} %select_n.41, bf16[4,3072]{1,0:T(4,128)(2,1)S(1)} %dynamic-slice_bitcast_fusion.2, bf16[256,3072]{1,0:T(8,128)(2,1)S(1)} %get-tuple-element.239, bf16[3072,1536]{1,0:T(8,128)(2,1)} %get-tuple-element.272, ...), kind=kOutput, calls=%fused_computation.12.clone.1 | convolution fusion | flops 808714240 | bytes 2648064 | tf_op jit(solution)/shard_map/while/body/eval_jaxpr/srk,kd->srd/dot_general | solution.py:78
  237.0 1.7 copy-done.2
  (45 shorter events, 0.5 us)
Async XLA Ops:
  6.5 46.4 %all-gather.5.cloned.1.call-start = ((), (), s32[]{:S(2)}) async-start(), calls=%async_computation.1 | async-start | bytes 3932160 | tf_op jit(solution)/shard_map/all_gather | solution.py:28
  7.3 89.8 %all-gather.3.cloned.1.call-start = ((), (), s32[]{:S(2)}) async-start(), calls=%async_computation | async-start | bytes 3932160 | tf_op jit(solution)/shard_map/all_gather | solution.py:27
  52.9 95.6 %collective-permute-start.4 = (bf16[16,64,1536]{2,1,0:T(8,128)(2,1)}, bf16[16,64,1536]{2,1,0:T(8,128)(2,1)S(1)}, u32[]{:S(2)}, u32[]{:S(2)}) collective-permute-start(bf16[16,64,1536]{2,1,0:T(8,128)(2,1)} %all-gather.5.cloned.1.call-done), channel_id=1, source_target_pairs={{0,1},{1,2},{2,3},{3,4},{4,5},{5,6},{6,7},{7,8},{8,9},{9,10},{10,1... | collective-permute-start | bytes 9437192 | tf_op jit(solution)/shard_map/ppermute | solution.py:12
  56.2 92.5 %collective-permute-start.5 = (bf16[16,64,1536]{2,1,0:T(8,128)(2,1)}, bf16[16,64,1536]{2,1,0:T(8,128)(2,1)}, u32[]{:S(2)}, u32[]{:S(2)}) collective-permute-start(bf16[16,64,1536]{2,1,0:T(8,128)(2,1)} %all-gather.5.cloned.1.call-done), channel_id=1, source_target_pairs={{0,63},{1,0},{2,1},{3,2},{4,3},{5,4},{6,5},{7,6},{8,7},{9,8},{10,9... | collective-permute-start | bytes 9437192 | tf_op jit(solution)/shard_map/ppermute | solution.py:12
  97.0 61.8 %collective-permute-start = (bf16[16,64,1536]{2,1,0:T(8,128)(2,1)}, bf16[16,64,1536]{2,1,0:T(8,128)(2,1)}, u32[]{:S(2)}, u32[]{:S(2)}) collective-permute-start(bf16[16,64,1536]{2,1,0:T(8,128)(2,1)} %all-gather.3.cloned.1.call-done), channel_id=1, source_target_pairs={{0,1},{1,2},{2,3},{3,4},{4,5},{5,6},{6,7},{7,8},{8,9},{9,10},{10,1... | collective-permute-start | bytes 9437192 | tf_op jit(solution)/shard_map/ppermute | solution.py:12
  100.2 58.5 %collective-permute-start.1 = (bf16[16,64,1536]{2,1,0:T(8,128)(2,1)}, bf16[16,64,1536]{2,1,0:T(8,128)(2,1)}, u32[]{:S(2)}, u32[]{:S(2)}) collective-permute-start(bf16[16,64,1536]{2,1,0:T(8,128)(2,1)} %all-gather.3.cloned.1.call-done), channel_id=1, source_target_pairs={{0,63},{1,0},{2,1},{3,2},{4,3},{5,4},{6,5},{7,6},{8,7},{9,8},{10,9... | collective-permute-start | bytes 9437192 | tf_op jit(solution)/shard_map/ppermute | solution.py:12
  110.8 26.0 %collective-permute-start.2 = (bf16[4,16,64,12]{2,0,3,1:T(4,128)(2,1)S(1)}, bf16[4,16,64,12]{2,0,3,1:T(4,128)(2,1)S(1)}, u32[]{:S(2)}, u32[]{:S(2)}) collective-permute-start(bf16[4,16,64,12]{2,0,3,1:T(4,128)(2,1)S(1)} %all_gather.10), channel_id=1, source_target_pairs={{0,1},{1,2},{2,3},{3,4},{4,5},{5,6},{6,7},{7,8},{8,9},{9,10},{10,1... | collective-permute-start | bytes 294920 | tf_op jit(solution)/shard_map/ppermute | solution.py:12
  136.8 7.1 %collective-permute-start.3 = (bf16[4,16,64,12]{2,0,3,1:T(4,128)(2,1)S(1)}, bf16[4,16,64,12]{2,0,3,1:T(4,128)(2,1)}, u32[]{:S(2)}, u32[]{:S(2)}) collective-permute-start(bf16[4,16,64,12]{2,0,3,1:T(4,128)(2,1)S(1)} %all_gather.10), channel_id=1, source_target_pairs={{0,63},{1,0},{2,1},{3,2},{4,3},{5,4},{6,5},{7,6},{8,7},{9,8},{10,9... | collective-permute-start | bytes 294920 | tf_op jit(solution)/shard_map/ppermute | solution.py:12
  148.6 1.7 copy-start.1
  150.3 8.5 %copy-start = (bf16[16,64,1536]{2,1,0:T(8,128)(2,1)S(1)}, bf16[16,64,1536]{2,1,0:T(8,128)(2,1)}, u32[]{:S(2)}) copy-start(bf16[16,64,1536]{2,1,0:T(8,128)(2,1)} %all-gather.3.cloned.1.call-done) | copy-start | bytes 9437188
  165.7 0.7 copy-start.3
  165.7 0.7 copy-start.4
  165.7 0.7 copy-start.5
  237.0 1.7 copy-start.2
Sparse Core Ops, SparseCore 0:
  9.1 43.7 all-gather.4
  54.8 42.2 all-gather.2
where the time goes:
time: 247 us; the launch traced here: 245 us
  waiting for transfers between devices  109 us (44%)
  matrix products  62.3 us (25%)
  other arithmetic  28.8 us (12%)
  between operations  13.5 us (5%)
  starting transfers between devices  12.1 us (5%)
  blocking collectives  9.6 us (4%)
  local copies, waits for them, and re-layouts  9.6 us (4%)
    all_gather x1, waiting for transfers between devices, per_device(): lax.all_gather(value_rows, 'tm', axis=0, tiled=True)  44.9 us
    all_gather x1, waiting for transfers between devices, per_device(): lax.all_gather(key_rows, 'tm', axis=0, tiled=True)  40.9 us
    dot_general x12, matrix products, one_head(): jnp.einsum('srk,kd->srd', dropped, value_h, preferred_element_type=jnp.fl...  36.4 us
    dot_general x12, matrix products, one_head(): jnp.einsum('rd,kd->rk', query_h, key_h, preferred_element_type=jnp.float32)  26 us
    ppermute x6, waiting for transfers between devices, from_behind(): lax.ppermute(shard, axis, [(i, (i + by) % peers) for i in range(peers)])  21.9 us
    ppermute x6, starting transfers between devices, from_behind(): lax.ppermute(shard, axis, [(i, (i + by) % peers) for i in range(peers)])  12 us
    all_gather x1, blocking collectives, per_device(): lax.all_gather(drop_low, 'tm', axis=1, tiled=True)  9.6 us
    another operation x1, other arithmetic, per_device(): window_values = jnp.stack(value_parts, axis=1)  8.52 us
  transfers between devices with their start and end apart: 8, of which 4 were waited for; matrix products, arithmetic and copies ran while one was open for 8% of the time, Pallas kernels for 0%

commit v1 on v0

--- a/solution.py
+++ b/solution.py
@@ -5,6 +5,13 @@
 from jax.sharding import PartitionSpec as P
 
 keep_rate = 0.9
+
+
+def exchange_gather(block, axis, d):
+    size = lax.axis_size(axis)
+    parts = jnp.stack([block for _ in range(size)])
+    parts = lax.all_to_all(parts, axis, split_axis=0, concat_axis=0)
+    return jnp.concatenate(parts, axis=d)
 
 
 def from_behind(shard, axis, by):
@@ -25,7 +32,7 @@
     drop_low = dropout.astype(jnp.bfloat16)
     all_keys, all_values, all_drops = (
         lax.all_gather(key_rows, "tm", axis=0, tiled=True),
-        lax.all_gather(value_rows, "tm", axis=0, tiled=True),
+        exchange_gather(value_rows, "tm", 0),
         lax.all_gather(drop_low, "tm", axis=1, tiled=True),
     )
     key_parts = [all_keys]

time: 247 us -> 257 us (1.040)
  blocking collectives: 9.6 us -> 71.6 us
  waiting for transfers between devices: 109 us -> 55 us
  starting transfers between devices: 12.1 us -> 16.5 us
    all_to_all x0 -> x1, blocking collectives: none -> 62.3 us  [exchange_gather(): parts = lax.all_to_all(parts, axis, split_axis=0, concat_axis=0)]
    all_gather x1 -> x0, waiting for transfers between devices: 44.9 us -> none  [per_device(): lax.all_gather(value_rows, 'tm', axis=0, tiled=True)]
    all_gather x1, waiting for transfers between devices: 40.9 us -> 0.01 us  [per_device(): lax.all_gather(key_rows, 'tm', axis=0, tiled=True)]
    ppermute x6, waiting for transfers between devices: 21.9 us -> 54.3 us  [from_behind(): lax.ppermute(shard, axis, [(i, (i + by) % peers) for i in range(peers)])]
    ppermute x6, starting transfers between devices: 12 us -> 16.5 us  [from_behind(): lax.ppermute(shard, axis, [(i, (i + by) % peers) for i in range(peers)])]
  transfers between devices with their start and end apart: 8 -> 7, of which waited for: 4 -> 2; matrix products, arithmetic and copies ran while one was open for 8% -> 7% of each run, Pallas kernels for 0% -> 0%
where the time goes in v1:
time: 257 us; the launch traced here: 256 us
  blocking collectives  71.6 us (28%)
  matrix products  62.4 us (24%)
  waiting for transfers between devices  55 us (21%)
  other arithmetic  27.1 us (11%)
  starting transfers between devices  16.5 us (6%)
  between operations  13.5 us (5%)
  local copies, waits for them, and re-layouts  9.35 us (4%)
    all_to_all x1, blocking collectives, exchange_gather(): parts = lax.all_to_all(parts, axis, split_axis=0, concat_axis=0)  62.3 us
    ppermute x6, waiting for transfers between devices, from_behind(): lax.ppermute(shard, axis, [(i, (i + by) % peers) for i in range(peers)])  54.3 us
    dot_general x12, matrix products, one_head(): jnp.einsum('srk,kd->srd', dropped, value_h, preferred_element_type=jnp.fl...  36.4 us
    dot_general x12, matrix products, one_head(): jnp.einsum('rd,kd->rk', query_h, key_h, preferred_element_type=jnp.float32)  26 us
    ppermute x6, starting transfers between devices, from_behind(): lax.ppermute(shard, axis, [(i, (i + by) % peers) for i in range(peers)])  16.5 us
    all_gather x1, blocking collectives, per_device(): lax.all_gather(drop_low, 'tm', axis=1, tiled=True)  9.31 us
    another operation x1, other arithmetic, per_device(): window_keys = jnp.stack(key_parts, axis=1)  8.4 us
    reduce_sum x12, other arithmetic, one_head(): total = jnp.sum(weight, axis=1)  7.42 us
  transfers between devices with their start and end apart: 7, of which 2 were waited for; matrix products, arithmetic and copies ran while one was open for 7% of the time, Pallas kernels for 0%

profile of v1, /device:TPU:97, one launch (start us, length us, event | category | flops | bytes accessed | tf_op | source)
XLA Modules:
  0.0 255.7 jit_solution(6274534782779789237)
XLA Ops:
  6.5 0.7 all-gather.2.cloned.1.call-update
  7.3 1.4 stack.64
  8.7 0.0 copy-start.1
  8.7 0.0 copy-start.5
  8.7 62.3 %all_to_all.5 = bf16[4,4,64,1536]{3,2,1,0:T(8,128)(2,1)S(1)} all-to-all(bf16[4,4,64,1536]{3,2,1,0:T(8,128)(2,1)S(1)} %stack.64), channel_id=1, replica_groups=mesh['tm'=4,'space'=64] {'tm'}, dimensions={0} | all-to-all | bytes 6291456 | tf_op jit(solution)/shard_map/all_to_all | solution.py:13
  71.0 7.7 %collective-permute-start.4 = (bf16[16,64,1536]{2,1,0:T(8,128)(2,1)S(1)}, bf16[16,64,1536]{2,1,0:T(8,128)(2,1)}, u32[]{:S(2)}, u32[]{:S(2)}) collective-permute-start(bf16[16,64,1536]{2,1,0:T(8,128)(2,1)S(1)} %bitcast.31), channel_id=1, source_target_pairs={{0,1},{1,2},{2,3},{3,4},{4,5},{5,6},{6,7},{7,8},{8,9},{9,10},{10,1... | collective-permute-start | bytes 9437192 | tf_op jit(solution)/shard_map/ppermute | solution.py:19
  78.8 3.0 %collective-permute-start = (bf16[16,64,1536]{2,1,0:T(8,128)(2,1)}, bf16[16,64,1536]{2,1,0:T(8,128)(2,1)}, u32[]{:S(2)}, u32[]{:S(2)}) collective-permute-start(bf16[16,64,1536]{2,1,0:T(8,128)(2,1)} %all-gather.2.cloned.1.call-done), channel_id=1, source_target_pairs={{0,1},{1,2},{2,3},{3,4},{4,5},{5,6},{6,7},{7,8},{8,9},{9,10},{10,1... | collective-permute-start | bytes 9437192 | tf_op jit(solution)/shard_map/ppermute | solution.py:19
  81.8 9.3 %all_gather.7 = bf16[4,16,64,12]{2,0,3,1:T(4,128)(2,1)S(1)} all-gather(bf16[4,4,64,12]{2,0,3,1:T(4,128)(2,1)S(1)} %copy_convert_fusion), channel_id=1, replica_groups=mesh['tm'=4,'space'=64] {'tm'}, dimensions={1}, use_global_device_ids=true | all-gather | bytes 122880 | tf_op jit(solution)/shard_map/all_gather | solution.py:36
  91.1 5.8 %collective-permute-start.2 = (bf16[4,16,64,12]{2,0,3,1:T(4,128)(2,1)S(1)}, bf16[4,16,64,12]{2,0,3,1:T(4,128)(2,1)S(1)}, u32[]{:S(2)}, u32[]{:S(2)}) collective-permute-start(bf16[4,16,64,12]{2,0,3,1:T(4,128)(2,1)S(1)} %all_gather.7), channel_id=1, source_target_pairs={{0,1},{1,2},{2,3},{3,4},{4,5},{5,6},{6,7},{7,8},{8,9},{9,10},{10,1... | collective-permute-start | bytes 294920 | tf_op jit(solution)/shard_map/ppermute | solution.py:19
  96.8 0.7 compare_reduce_fusion.2
  97.5 2.0 pad_add_fusion
  99.5 0.1 broadcast_in_dim.36
  99.6 0.1 tile.7
  99.7 0.7 and.23
  100.4 48.4 %collective-permute-done.2 = bf16[4,16,64,12]{2,0,3,1:T(4,128)(2,1)S(1)} collective-permute-done((bf16[4,16,64,12]{2,0,3,1:T(4,128)(2,1)S(1)}, bf16[4,16,64,12]{2,0,3,1:T(4,128)(2,1)S(1)}, u32[]{:S(2)}, u32[]{:S(2)}) %collective-permute-start.2) | collective-permute-done | bytes 98336 | tf_op jit(solution)/shard_map/ppermute | solution.py:19
  148.8 0.6 add.56
  149.4 0.7 le.15
  150.1 5.8 %collective-permute-done.3 = bf16[4,16,64,12]{2,0,3,1:T(4,128)(2,1)} collective-permute-done((bf16[4,16,64,12]{2,0,3,1:T(4,128)(2,1)S(1)}, bf16[4,16,64,12]{2,0,3,1:T(4,128)(2,1)}, u32[]{:S(2)}, u32[]{:S(2)}) %collective-permute-start.3) | collective-permute-done | bytes 98336 | tf_op jit(solution)/shard_map/ppermute | solution.py:19
  155.9 1.5 pad_maximum_fusion.2
  157.4 1.4 copy.16
  158.8 1.8 reshape.48
  160.6 7.0 %pad_maximum_fusion.1 = bf16[16,3,64,1536]{3,2,1,0:T(8,128)(2,1)} fusion(bf16[16,1,64,1536]{3,2,1,0:T(8,128)(2,1)} %bitcast.13, bf16[16,1,64,1536]{3,2,1,0:T(8,128)(2,1)} %bitcast.12, bf16[16,1,64,1536]{3,2,1,0:T(8,128)(2,1)S(1)} %bitcast.33), kind=kLoop, calls=%fused_computation.22 | loop fusion | flops 9437184 | bytes 18874368 | tf_op jit(solution)/shard_map/stack | solution.py:51
  167.6 8.4 %pad_maximum_fusion = bf16[16,3,64,1536]{3,2,1,0:T(8,128)(2,1)} fusion(bf16[16,1,64,1536]{3,2,1,0:T(8,128)(2,1)} %bitcast.3, bf16[16,1,64,1536]{3,2,1,0:T(8,128)(2,1)} %bitcast.2, bf16[16,1,64,1536]{3,2,1,0:T(8,128)(2,1)} %bitcast.36), kind=kLoop, calls=%fused_computation.21 | loop fusion | flops 9437184 | bytes 18874368 | tf_op jit(solution)/shard_map/stack | solution.py:50
  176.0 0.2 broadcast_in_dim.33
  176.2 0.5 copy-done.2
  176.7 70.5 %while.14 = (s32[]{:T(128)}, bf16[4,256,1536]{2,1,0:T(8,128)(2,1)S(1)}, bf16[256,1536]{1,0:T(8,128)(2,1)}, bf16[3072,1536]{1,0:T(8,128)(2,1)}, bf16[12,4,3072]{2...) while((s32[]{:T(128)}, ...), condition=%wide.region_6.7_spmd.clone, body=%wide.region_3.6_spmd.clone.sunk | while | flops 1016332032 | bytes 11436207 | solution.py:90
  176.7 2.2 fusion.32
  178.9 0.6 fusion.33
  179.5 3.0 %fusion.34 = bf16[4,256,1536]{2,1,0:T(8,128)(2,1)S(1)} fusion(bf16[4,256,1536]{2,1,0:T(8,128)(2,1)S(1)} %get-tuple-element.255, s32[]{:T(128)S(6)} %select_n.41, bf16[4,3072]{1,0:T(4,128)(2,1)S(1)} %dynamic-slice_bitcast_fusion.2, bf16[256,3072]{1,0:T(8,128)(2,1)S(1)} %get-tuple-element.239, bf16[3072,1536]{1,0:T(8,128)(2,1)} %get-tuple-element.272, ...), kind=kOutput, calls=%fused_computation.12.clone.1 | convolution fusion | flops 808714240 | bytes 2648064 | tf_op jit(solution)/shard_map/while/body/eval_jaxpr/srk,kd->srd/dot_general | solution.py:85
  182.6 2.2 fusion.32
  184.7 0.6 fusion.33
  185.4 3.0 %fusion.34 = bf16[4,256,1536]{2,1,0:T(8,128)(2,1)S(1)} fusion(bf16[4,256,1536]{2,1,0:T(8,128)(2,1)S(1)} %get-tuple-element.255, s32[]{:T(128)S(6)} %select_n.41, bf16[4,3072]{1,0:T(4,128)(2,1)S(1)} %dynamic-slice_bitcast_fusion.2, bf16[256,3072]{1,0:T(8,128)(2,1)S(1)} %get-tuple-element.239, bf16[3072,1536]{1,0:T(8,128)(2,1)} %get-tuple-element.272, ...), kind=kOutput, calls=%fused_computation.12.clone.1 | convolution fusion | flops 808714240 | bytes 2648064 | tf_op jit(solution)/shard_map/while/body/eval_jaxpr/srk,kd->srd/dot_general | solution.py:85
  188.4 2.2 fusion.32
  190.6 0.6 fusion.33
  191.3 3.0 %fusion.34 = bf16[4,256,1536]{2,1,0:T(8,128)(2,1)S(1)} fusion(bf16[4,256,1536]{2,1,0:T(8,128)(2,1)S(1)} %get-tuple-element.255, s32[]{:T(128)S(6)} %select_n.41, bf16[4,3072]{1,0:T(4,128)(2,1)S(1)} %dynamic-slice_bitcast_fusion.2, bf16[256,3072]{1,0:T(8,128)(2,1)S(1)} %get-tuple-element.239, bf16[3072,1536]{1,0:T(8,128)(2,1)} %get-tuple-element.272, ...), kind=kOutput, calls=%fused_computation.12.clone.1 | convolution fusion | flops 808714240 | bytes 2648064 | tf_op jit(solution)/shard_map/while/body/eval_jaxpr/srk,kd->srd/dot_general | solution.py:85
  194.3 2.2 fusion.32
  196.5 0.6 fusion.33
  197.1 3.0 %fusion.34 = bf16[4,256,1536]{2,1,0:T(8,128)(2,1)S(1)} fusion(bf16[4,256,1536]{2,1,0:T(8,128)(2,1)S(1)} %get-tuple-element.255, s32[]{:T(128)S(6)} %select_n.41, bf16[4,3072]{1,0:T(4,128)(2,1)S(1)} %dynamic-slice_bitcast_fusion.2, bf16[256,3072]{1,0:T(8,128)(2,1)S(1)} %get-tuple-element.239, bf16[3072,1536]{1,0:T(8,128)(2,1)} %get-tuple-element.272, ...), kind=kOutput, calls=%fused_computation.12.clone.1 | convolution fusion | flops 808714240 | bytes 2648064 | tf_op jit(solution)/shard_map/while/body/eval_jaxpr/srk,kd->srd/dot_general | solution.py:85
  200.2 2.2 fusion.32
  202.4 0.6 fusion.33
  203.0 3.0 %fusion.34 = bf16[4,256,1536]{2,1,0:T(8,128)(2,1)S(1)} fusion(bf16[4,256,1536]{2,1,0:T(8,128)(2,1)S(1)} %get-tuple-element.255, s32[]{:T(128)S(6)} %select_n.41, bf16[4,3072]{1,0:T(4,128)(2,1)S(1)} %dynamic-slice_bitcast_fusion.2, bf16[256,3072]{1,0:T(8,128)(2,1)S(1)} %get-tuple-element.239, bf16[3072,1536]{1,0:T(8,128)(2,1)} %get-tuple-element.272, ...), kind=kOutput, calls=%fused_computation.12.clone.1 | convolution fusion | flops 808714240 | bytes 2648064 | tf_op jit(solution)/shard_map/while/body/eval_jaxpr/srk,kd->srd/dot_general | solution.py:85
  206.1 2.2 fusion.32
  208.2 0.6 fusion.33
  208.9 3.0 %fusion.34 = bf16[4,256,1536]{2,1,0:T(8,128)(2,1)S(1)} fusion(bf16[4,256,1536]{2,1,0:T(8,128)(2,1)S(1)} %get-tuple-element.255, s32[]{:T(128)S(6)} %select_n.41, bf16[4,3072]{1,0:T(4,128)(2,1)S(1)} %dynamic-slice_bitcast_fusion.2, bf16[256,3072]{1,0:T(8,128)(2,1)S(1)} %get-tuple-element.239, bf16[3072,1536]{1,0:T(8,128)(2,1)} %get-tuple-element.272, ...), kind=kOutput, calls=%fused_computation.12.clone.1 | convolution fusion | flops 808714240 | bytes 2648064 | tf_op jit(solution)/shard_map/while/body/eval_jaxpr/srk,kd->srd/dot_general | solution.py:85
  212.0 2.2 fusion.32
  214.1 0.6 fusion.33
  214.8 3.0 %fusion.34 = bf16[4,256,1536]{2,1,0:T(8,128)(2,1)S(1)} fusion(bf16[4,256,1536]{2,1,0:T(8,128)(2,1)S(1)} %get-tuple-element.255, s32[]{:T(128)S(6)} %select_n.41, bf16[4,3072]{1,0:T(4,128)(2,1)S(1)} %dynamic-slice_bitcast_fusion.2, bf16[256,3072]{1,0:T(8,128)(2,1)S(1)} %get-tuple-element.239, bf16[3072,1536]{1,0:T(8,128)(2,1)} %get-tuple-element.272, ...), kind=kOutput, calls=%fused_computation.12.clone.1 | convolution fusion | flops 808714240 | bytes 2648064 | tf_op jit(solution)/shard_map/while/body/eval_jaxpr/srk,kd->srd/dot_general | solution.py:85
  217.8 2.2 fusion.32
  220.0 0.6 fusion.33
  220.7 3.0 %fusion.34 = bf16[4,256,1536]{2,1,0:T(8,128)(2,1)S(1)} fusion(bf16[4,256,1536]{2,1,0:T(8,128)(2,1)S(1)} %get-tuple-element.255, s32[]{:T(128)S(6)} %select_n.41, bf16[4,3072]{1,0:T(4,128)(2,1)S(1)} %dynamic-slice_bitcast_fusion.2, bf16[256,3072]{1,0:T(8,128)(2,1)S(1)} %get-tuple-element.239, bf16[3072,1536]{1,0:T(8,128)(2,1)} %get-tuple-element.272, ...), kind=kOutput, calls=%fused_computation.12.clone.1 | convolution fusion | flops 808714240 | bytes 2648064 | tf_op jit(solution)/shard_map/while/body/eval_jaxpr/srk,kd->srd/dot_general | solution.py:85
  223.7 2.2 fusion.32
  225.9 0.6 fusion.33
  226.5 3.0 %fusion.34 = bf16[4,256,1536]{2,1,0:T(8,128)(2,1)S(1)} fusion(bf16[4,256,1536]{2,1,0:T(8,128)(2,1)S(1)} %get-tuple-element.255, s32[]{:T(128)S(6)} %select_n.41, bf16[4,3072]{1,0:T(4,128)(2,1)S(1)} %dynamic-slice_bitcast_fusion.2, bf16[256,3072]{1,0:T(8,128)(2,1)S(1)} %get-tuple-element.239, bf16[3072,1536]{1,0:T(8,128)(2,1)} %get-tuple-element.272, ...), kind=kOutput, calls=%fused_computation.12.clone.1 | convolution fusion | flops 808714240 | bytes 2648064 | tf_op jit(solution)/shard_map/while/body/eval_jaxpr/srk,kd->srd/dot_general | solution.py:85
  229.6 2.2 fusion.32
  231.8 0.6 fusion.33
  232.4 3.0 %fusion.34 = bf16[4,256,1536]{2,1,0:T(8,128)(2,1)S(1)} fusion(bf16[4,256,1536]{2,1,0:T(8,128)(2,1)S(1)} %get-tuple-element.255, s32[]{:T(128)S(6)} %select_n.41, bf16[4,3072]{1,0:T(4,128)(2,1)S(1)} %dynamic-slice_bitcast_fusion.2, bf16[256,3072]{1,0:T(8,128)(2,1)S(1)} %get-tuple-element.239, bf16[3072,1536]{1,0:T(8,128)(2,1)} %get-tuple-element.272, ...), kind=kOutput, calls=%fused_computation.12.clone.1 | convolution fusion | flops 808714240 | bytes 2648064 | tf_op jit(solution)/shard_map/while/body/eval_jaxpr/srk,kd->srd/dot_general | solution.py:85
  235.5 2.2 fusion.32
  237.6 0.6 fusion.33
  238.3 3.0 %fusion.34 = bf16[4,256,1536]{2,1,0:T(8,128)(2,1)S(1)} fusion(bf16[4,256,1536]{2,1,0:T(8,128)(2,1)S(1)} %get-tuple-element.255, s32[]{:T(128)S(6)} %select_n.41, bf16[4,3072]{1,0:T(4,128)(2,1)S(1)} %dynamic-slice_bitcast_fusion.2, bf16[256,3072]{1,0:T(8,128)(2,1)S(1)} %get-tuple-element.239, bf16[3072,1536]{1,0:T(8,128)(2,1)} %get-tuple-element.272, ...), kind=kOutput, calls=%fused_computation.12.clone.1 | convolution fusion | flops 808714240 | bytes 2648064 | tf_op jit(solution)/shard_map/while/body/eval_jaxpr/srk,kd->srd/dot_general | solution.py:85
  241.3 2.2 fusion.32
  243.5 0.6 fusion.33
  244.2 3.0 %fusion.34 = bf16[4,256,1536]{2,1,0:T(8,128)(2,1)S(1)} fusion(bf16[4,256,1536]{2,1,0:T(8,128)(2,1)S(1)} %get-tuple-element.255, s32[]{:T(128)S(6)} %select_n.41, bf16[4,3072]{1,0:T(4,128)(2,1)S(1)} %dynamic-slice_bitcast_fusion.2, bf16[256,3072]{1,0:T(8,128)(2,1)S(1)} %get-tuple-element.239, bf16[3072,1536]{1,0:T(8,128)(2,1)} %get-tuple-element.272, ...), kind=kOutput, calls=%fused_computation.12.clone.1 | convolution fusion | flops 808714240 | bytes 2648064 | tf_op jit(solution)/shard_map/while/body/eval_jaxpr/srk,kd->srd/dot_general | solution.py:85
  247.2 0.0 copy-start
  247.2 1.7 copy-done
  (44 shorter events, 0.4 us)
Async XLA Ops:
  6.5 72.2 %all-gather.2.cloned.1.call-start = ((), (), s32[]{:S(2)}) async-start(), calls=%async_computation.1 | async-start | bytes 3932160 | tf_op jit(solution)/shard_map/all_gather | solution.py:34
  8.7 73.0 %copy-start.1 = (s32[4,4,64,12]{2,1,3,0:T(4,128)S(1)}, s32[4,4,64,12]{2,1,3,0:T(4,128)}, u32[]{:S(2)}) copy-start(s32[4,4,64,12]{2,1,3,0:T(4,128)} %param.10) | copy-start | bytes 147460
  8.7 88.1 %copy-start.5 = (s32[1,2]{1,0:T(1,128)S(1)}, s32[1,2]{1,0:T(1,128)}, u32[]{:S(2)}) copy-start(s32[1,2]{1,0:T(1,128)} %param.11) | copy-start | bytes 28
  71.0 89.6 %collective-permute-start.4 = (bf16[16,64,1536]{2,1,0:T(8,128)(2,1)S(1)}, bf16[16,64,1536]{2,1,0:T(8,128)(2,1)}, u32[]{:S(2)}, u32[]{:S(2)}) collective-permute-start(bf16[16,64,1536]{2,1,0:T(8,128)(2,1)S(1)} %bitcast.31), channel_id=1, source_target_pairs={{0,1},{1,2},{2,3},{3,4},{4,5},{5,6},{6,7},{7,8},{8,9},{9,10},{10,1... | collective-permute-start | bytes 9437192 | tf_op jit(solution)/shard_map/ppermute | solution.py:19
  78.8 81.8 %collective-permute-start.5 = (bf16[16,64,1536]{2,1,0:T(8,128)(2,1)S(1)}, bf16[16,64,1536]{2,1,0:T(8,128)(2,1)}, u32[]{:S(2)}, u32[]{:S(2)}) collective-permute-start(bf16[16,64,1536]{2,1,0:T(8,128)(2,1)S(1)} %bitcast.32), channel_id=1, source_target_pairs={{0,63},{1,0},{2,1},{3,2},{4,3},{5,4},{6,5},{7,6},{8,7},{9,8},{10,9... | collective-permute-start | bytes 9437192 | tf_op jit(solution)/shard_map/ppermute | solution.py:19
  78.8 88.8 %collective-permute-start = (bf16[16,64,1536]{2,1,0:T(8,128)(2,1)}, bf16[16,64,1536]{2,1,0:T(8,128)(2,1)}, u32[]{:S(2)}, u32[]{:S(2)}) collective-permute-start(bf16[16,64,1536]{2,1,0:T(8,128)(2,1)} %all-gather.2.cloned.1.call-done), channel_id=1, source_target_pairs={{0,1},{1,2},{2,3},{3,4},{4,5},{5,6},{6,7},{7,8},{8,9},{9,10},{10,1... | collective-permute-start | bytes 9437192 | tf_op jit(solution)/shard_map/ppermute | solution.py:19
  81.7 85.9 %collective-permute-start.1 = (bf16[16,64,1536]{2,1,0:T(8,128)(2,1)}, bf16[16,64,1536]{2,1,0:T(8,128)(2,1)}, u32[]{:S(2)}, u32[]{:S(2)}) collective-permute-start(bf16[16,64,1536]{2,1,0:T(8,128)(2,1)} %all-gather.2.cloned.1.call-done), channel_id=1, source_target_pairs={{0,63},{1,0},{2,1},{3,2},{4,3},{5,4},{6,5},{7,6},{8,7},{9,8},{10,9... | collective-permute-start | bytes 9437192 | tf_op jit(solution)/shard_map/ppermute | solution.py:19
  91.1 57.7 %collective-permute-start.2 = (bf16[4,16,64,12]{2,0,3,1:T(4,128)(2,1)S(1)}, bf16[4,16,64,12]{2,0,3,1:T(4,128)(2,1)S(1)}, u32[]{:S(2)}, u32[]{:S(2)}) collective-permute-start(bf16[4,16,64,12]{2,0,3,1:T(4,128)(2,1)S(1)} %all_gather.7), channel_id=1, source_target_pairs={{0,1},{1,2},{2,3},{3,4},{4,5},{5,6},{6,7},{7,8},{8,9},{9,10},{10,1... | collective-permute-start | bytes 294920 | tf_op jit(solution)/shard_map/ppermute | solution.py:19
  148.8 7.1 %collective-permute-start.3 = (bf16[4,16,64,12]{2,0,3,1:T(4,128)(2,1)S(1)}, bf16[4,16,64,12]{2,0,3,1:T(4,128)(2,1)}, u32[]{:S(2)}, u32[]{:S(2)}) collective-permute-start(bf16[4,16,64,12]{2,0,3,1:T(4,128)(2,1)S(1)} %all_gather.7), channel_id=1, source_target_pairs={{0,63},{1,0},{2,1},{3,2},{4,3},{5,4},{6,5},{7,6},{8,7},{9,8},{10,9... | collective-permute-start | bytes 294920 | tf_op jit(solution)/shard_map/ppermute | solution.py:19
  176.0 0.7 copy-start.2
  176.0 0.7 copy-start.3
  176.0 0.7 copy-start.4
  247.2 1.7 copy-start
Sparse Core Ops, SparseCore 0:
  9.1 67.0 all-gather.1
